TPU v7x, 32 devices: a whole 2x2x4 slice. The times are simulated.
32 devices in a mesh: groups: 2 (over y), latent: 8 (over z, x), hidden: 2 (over core).
Axes of the slice: x: 2, y: 2, z: 4, core: 2. Of those that a mesh axis runs over, the one named last changes fastest.
Arguments:
- input_codes: int32 [288, 2304], P('groups', ('latent', 'hidden')), parts along dimension 0, may hold values from -128 to 127
- cotangent_codes: int32 [288, 2304], P('groups', ('latent', 'hidden')), parts along dimension 0, may hold values from -128 to 127
- dictionary: bfloat16 [8192, 2304], P(('latent', 'hidden')), as said below
- encoder_bias: float32 [8192], P(('latent', 'hidden')), may hold values from -12 to 0, as said below
- decoder_bias: float32 [2304], replicated, may hold values from -1.2 to 1.2
- norm_gain: float32 [2304], replicated, may hold values from 0.1 to 1.9
- gate_weight: bfloat16 [8192, 2304], P(('latent', 'hidden')), may hold values from -0.1875 to 0.1875
- up_weight: bfloat16 [8192, 2304], P(('latent', 'hidden')), may hold values from -0.1875 to 0.1875
- down_weight: bfloat16 [8192, 2304], P(('latent', 'hidden')), may hold values from -0.09375 to 0.09375
Outputs:
- block_output: bfloat16 [288, 2304], P('groups', ('latent', 'hidden')), parts along dimension 0
- dictionary_grad: bfloat16 [8192, 4608], P(('latent', 'hidden'), 'groups'), parts along dimension 1
There are 2 independent parts, one for each index of `groups`. A program takes and returns all parts, laid end to end along the dimension named above; an argument that names none is the same for every part. Nothing has to cross between parts.
Inputs may be any that keep to these rules, and one draw needn't show every extreme that they name: `dictionary`: every entry is a whole multiple of 2^-10, at most 119 such units in magnitude. `encoder_bias`: every entry is a whole multiple of 2^-16.
All inputs are finite; a program needn't handle non-finite values.
Results may differ from a plain program's by a relative error of at most 0.0072.
Values may be sent and summed in bfloat16 or wider, within the bound.
A program may use at most 64 MiB of HBM per device.

v0:
```python
import jax
import jax.numpy as jnp
from jax import lax
from jax.sharding import PartitionSpec as P

CODE_STEP = 2.0 ** (-6)
NORM_EPSILON = 1e-06
GELU_ROOT = 0.7978845608028654
GELU_CUBIC = 0.044715
ACROSS = (((1,), (1,)), ((), ()))
DOWNWARD = (((0,), (0,)), ((), ()))


def gelu_parts(values):
    argument = GELU_ROOT * (values + GELU_CUBIC * values * values * values)
    tanh_value = jnp.tanh(argument)
    result = 0.5 * values * (1.0 + tanh_value)
    derivative = 0.5 * (1.0 + tanh_value) + 0.5 * values * (
        1.0 - tanh_value * tanh_value
    ) * GELU_ROOT * (1.0 + 3.0 * GELU_CUBIC * values * values)
    return (result, derivative)


def per_device(
    input_codes,
    cotangent_codes,
    dictionary,
    encoder_bias,
    decoder_bias,
    norm_gain,
    gate_weight,
    up_weight,
    down_weight,
):
    own_width = input_codes.shape[1]
    model_width = own_width * lax.axis_size(("latent", "hidden"))
    cotangent_local = (cotangent_codes.astype(jnp.float32) * CODE_STEP).astype(jnp.bfloat16)
    hidden_grad = None
    inputs_local = (input_codes.astype(jnp.float32) * CODE_STEP).astype(jnp.bfloat16)
    inputs = lax.all_gather(inputs_local, ("latent", "hidden"), axis=1, tiled=True)
    preact = (
        lax.dot_general(inputs, dictionary, ACROSS, preferred_element_type=jnp.float32)
        + encoder_bias
    )
    latents = jnp.maximum(preact, 0.0).astype(jnp.bfloat16)
    partial_value = jnp.dot(latents, dictionary, preferred_element_type=jnp.float32)
    rebuilt = lax.psum(partial_value, ("latent", "hidden")) + decoder_bias
    inverse = lax.rsqrt(
        jnp.sum(rebuilt * rebuilt, axis=1, keepdims=True) / model_width + NORM_EPSILON
    )
    normed = (rebuilt * inverse * norm_gain).astype(jnp.bfloat16)
    target = inputs.astype(jnp.float32)
    gate_proj = lax.dot_general(normed, gate_weight, ACROSS, preferred_element_type=jnp.float32)
    up_proj = lax.dot_general(normed, up_weight, ACROSS, preferred_element_type=jnp.float32)
    gelu_value, gelu_slope = gelu_parts(gate_proj)
    hidden = (gelu_value * up_proj).astype(jnp.bfloat16)
    output_terms = jnp.dot(hidden, down_weight, preferred_element_type=jnp.float32)
    block_output = lax.psum_scatter(
        output_terms, ("latent", "hidden"), scatter_dimension=1, tiled=True
    ).astype(jnp.bfloat16)
    hidden_grad = lax.dot_general(
        lax.all_gather(cotangent_local, ("latent", "hidden"), axis=1, tiled=True),
        down_weight,
        ACROSS,
        preferred_element_type=jnp.float32,
    )
    gate_grad = (hidden_grad * up_proj * gelu_slope).astype(jnp.bfloat16)
    up_grad = (hidden_grad * gelu_value).astype(jnp.bfloat16)
    partial_grad = jnp.dot(gate_grad, gate_weight, preferred_element_type=jnp.float32) + jnp.dot(
        up_grad, up_weight, preferred_element_type=jnp.float32
    )
    scaled = lax.psum(partial_grad, ("latent", "hidden")) * norm_gain
    inner_row = jnp.sum(scaled * rebuilt, axis=1, keepdims=True)
    inverse_cube = inverse * inverse * inverse
    rebuilt_grad = (
        inverse * scaled - inverse_cube * rebuilt * (inner_row / model_width) + (rebuilt - target)
    ).astype(jnp.bfloat16)
    latent_grad = lax.dot_general(
        rebuilt_grad, dictionary, ACROSS, preferred_element_type=jnp.float32
    )
    preact_grad = jnp.where(preact > 0.0, latent_grad, 0.0).astype(jnp.bfloat16)
    dictionary_grad = lax.dot_general(
        latents, rebuilt_grad, DOWNWARD, preferred_element_type=jnp.float32
    ) + lax.dot_general(preact_grad, inputs, DOWNWARD, preferred_element_type=jnp.float32)
    return (block_output, dictionary_grad.astype(jnp.bfloat16))


def solution(mesh):
    in_specs = (
        P("groups", ("latent", "hidden")),
        P("groups", ("latent", "hidden")),
        P(("latent", "hidden"), None),
        P(("latent", "hidden")),
        P(),
        P(),
        P(("latent", "hidden"), None),
        P(("latent", "hidden"), None),
        P(("latent", "hidden"), None),
    )
    out_specs = (P("groups", ("latent", "hidden")), P(("latent", "hidden"), "groups"))
    return jax.shard_map(
        per_device, mesh=mesh, in_specs=in_specs, out_specs=out_specs, check_vma=False
    )
```

profile of v0, /device:TPU:0, one launch (start us, length us, event | category | flops | bytes accessed | tf_op | source)
XLA Modules:
  0.0 309.8 jit_solution(10657653489420089251)
XLA Ops:
  7.2 1.2 copy.11
  8.4 26.4 %all_gather.6 = bf16[144,2304]{0,1:T(8,128)(2,1)S(1)} all-gather(bf16[144,144]{0,1:T(8,128)(2,1)S(1)} %multiply_convert_fusion.6), channel_id=1, replica_groups=mesh['groups'=2,'latent'=8,'hidden'=2] {'latent','hidden'}, dimensions={1}, use_global_device_ids=true | all-gather | bytes 705024 | tf_op jit(solution)/shard_map/all_gather | solution.py:40
  34.8 0.9 convolution_add_fusion.2
  35.8 0.7 copy-done.8
  36.5 1.6 fusion.19
  38.1 1.7 copy.12
  39.8 0.9 multiply_convert_fusion.5
  40.7 24.5 %all_gather.7 = bf16[144,2304]{0,1:T(8,128)(2,1)S(1)} all-gather(bf16[144,144]{0,1:T(8,128)(2,1)S(1)} %multiply_convert_fusion.5), channel_id=1, replica_groups=mesh['groups'=2,'latent'=8,'hidden'=2] {'latent','hidden'}, dimensions={1}, use_global_device_ids=true | all-gather | bytes 705024 | tf_op jit(solution)/shard_map/all_gather | solution.py:62
  65.3 3.4 %fusion.38 = f32[144,512]{1,0:T(8,128)} fusion(bf16[144,2304]{0,1:T(8,128)(2,1)S(1)} %all_gather.7, bf16[512,2304]{1,0:T(8,128)(2,1)} %param.17), kind=kOutput, calls=%fused_computation.57 | convolution fusion | flops 339738624 | bytes 3317760 | tf_op jit(solution)/shard_map/dot_general | solution.py:61
  68.6 63.1 %all-reduce.3.cloned.1.call-done = f32[144,2304]{1,0:T(8,128)} async-done(((f32[144,2304]{1,0:T(8,128)}), f32[144,2304]{1,0:T(8,128)}) %all-reduce.3.cloned.1.call-update) | async-done | bytes 1327120 | tf_op jit(solution)/shard_map/psum | solution.py:47
  131.7 1.6 multiply_reduce_fusion.1
  133.9 2.8 fusion.37
  136.7 0.9 fusion.36
  137.7 0.8 copy-done.3
  139.2 1.7 convolution_add_fusion.1
  141.0 1.3 copy.13
  142.2 4.4 %convolution_bitcast_fusion = f32[2304,144]{1,0:T(8,128)} fusion(bf16[512,2304]{1,0:T(8,128)(2,1)} %param.17, f32[144,512]{1,0:T(8,128)} %copy-done.7, f32[144,512]{1,0:T(8,128)} %copy-done.5), kind=kOutput, calls=%fused_computation.2 | convolution fusion | flops 340475904 | bytes 4276224
  146.6 88.4 %all-reduce.5.cloned.1.call-done = f32[144,2304]{1,0:T(8,128)} async-done(((f32[144,2304]{1,0:T(8,128)}), f32[144,2304]{1,0:T(8,128)}) %all-reduce.5.cloned.1.call-update) | async-done | bytes 1327120 | tf_op jit(solution)/shard_map/psum | solution.py:72
  235.0 2.1 multiply_reduce_fusion
  237.5 2.5 add_convert_fusion
  240.0 5.1 %fusion.2 = f32[512,2304]{1,0:T(8,128)} fusion(bf16[144,2304]{0,1:T(8,128)(2,1)S(1)} %all_gather.6, bf16[144,2304]{1,0:T(8,128)(2,1)} %add_convert_fusion, bf16[512,2304]{1,0:T(8,128)(2,1)S(1)} %copy-done, f32[144,512]{1,0:T(8,128)} %copy-done.8), kind=kOutput, calls=%fused_computation.11 | convolution fusion | flops 679698432 | bytes 8699904 | tf_op jit(solution)/shard_map/dot_general | solution.py:84
  245.1 5.1 %fusion = bf16[512,2304]{1,0:T(8,128)(2,1)} fusion(f32[512,2304]{1,0:T(8,128)} %fusion.2, bf16[144,2304]{1,0:T(8,128)(2,1)} %add_convert_fusion, f32[144,512]{1,0:T(8,128)} %copy-done.8), kind=kOutput, calls=%fused_computation.1 | convolution fusion | flops 342245376 | bytes 8036352 | tf_op jit(solution)/shard_map/dot_general | solution.py:82
  250.2 51.5 %reduce-scatter.4.cloned.1.call-done = f32[144,144]{1,0:T(8,128)} async-done(((f32[2304,144]{1,0:T(8,128)}), f32[144,144]{1,0:T(8,128)}) %reduce-scatter.4.cloned.1.call-update) | async-done | bytes 82960
  301.7 1.6 copy.15
  (38 shorter events, 1.9 us)
Async XLA Ops:
  7.2 27.7 %copy-start = (bf16[512,2304]{1,0:T(8,128)(2,1)S(1)}, bf16[512,2304]{1,0:T(8,128)(2,1)}, u32[]{:S(2)}) copy-start(bf16[512,2304]{1,0:T(8,128)(2,1)} %param.11) | copy-start | bytes 7077892
  7.2 27.7 %copy-start.14 = (f32[512]{0:T(512)S(1)}, f32[512]{0:T(512)}, u32[]{:S(2)}) copy-start(f32[512]{0:T(512)} %param.12) | copy-start | bytes 6148
  7.2 124.5 %all-reduce.3.cloned.1.call-start = ((), (), s32[]{:S(2)}) async-start(), calls=%async_computation.1 | async-start | bytes 2654208 | tf_op jit(solution)/shard_map/psum | solution.py:47
  35.8 0.7 copy-start.8
  38.1 196.9 %all-reduce.5.cloned.1.call-start = ((), (), s32[]{:S(2)}) async-start(), calls=%async_computation.2 | async-start | bytes 2654208 | tf_op jit(solution)/shard_map/psum | solution.py:72
  65.3 66.4 %copy-start.10 = (f32[2304]{0:T(1024)S(1)}, f32[2304]{0:T(1024)}, u32[]{:S(2)}) copy-start(f32[2304]{0:T(1024)} %param.13) | copy-start | bytes 27652
  131.7 2.2 copy-start.1
  131.7 2.2 copy-start.11
  133.9 2.8 copy-start.4
  136.7 2.5 copy-start.5
  136.7 1.8 copy-start.3
  136.7 1.8 copy-start.9
  138.5 0.7 copy-start.7
  140.9 160.8 %reduce-scatter.4.cloned.1.call-start = ((), (), s32[]{:S(2)}) async-start(), calls=%async_computation.3 | async-start | bytes 2506752
  235.0 2.2 copy-start.2
  235.0 2.5 copy-start.6
  235.0 2.5 copy-start.12
  235.0 2.5 copy-start.13
Sparse Core Ops, SparseCore 0:
  38.2 93.4 all-reduce.2
  141.0 93.9 all-reduce.4
  238.7 62.8 reduce-scatter.3
where the time goes:
time: 310 us
  waiting for transfers between devices  203 us (65%)
  blocking collectives  50.9 us (16%)
  matrix products  26.4 us (9%)
  between operations  13.9 us (4%)
  other arithmetic  7.82 us (3%)
  local copies, waits for them, and re-layouts  7.76 us (3%)
    psum x1, waiting for transfers between devices, per_device(): scaled = lax.psum(partial_grad, ('latent', 'hidden')) * norm_gain  88.4 us
    psum x1, waiting for transfers between devices, per_device(): rebuilt = lax.psum(partial_value, ('latent', 'hidden')) + decoder_bias  63.1 us
    unnamed x4, waiting for transfers between devices  51.5 us
    all_gather x1, blocking collectives, per_device(): lax.all_gather(inputs_local, ('latent', 'hidden'), axis=1, tiled=True)  26.4 us
    all_gather x1, blocking collectives, per_device(): lax.all_gather(cotangent_local, ('latent', 'hidden'), axis=1, tiled=True)  24.5 us
    unnamed x33, local copies, waits for them, and re-layouts  6.49 us
  transfers between devices with their start and end apart: 3, of which 3 were waited for; matrix products, arithmetic and copies ran while one was open for 9% of the time, Pallas kernels for 0%

commit v1 on v0

--- a/solution.py
+++ b/solution.py
@@ -1,7 +1,534 @@
+import types
+
 import jax
 import jax.numpy as jnp
 from jax import lax
+from jax.experimental import pallas as pl
+from jax.experimental.pallas import tpu as pltpu
 from jax.sharding import PartitionSpec as P
+
+ROWS = 8
+LANES = 128
+TILE = 256
+MESH = pl.DeviceIdType.MESH
+F32 = jnp.float32
+BF16 = jnp.bfloat16
+
+
+def group_kernel(L, H, refs_in, refs_out, s):
+    (codes_x, codes_u, dic_hbm, ebias, dbias, gain, gate_hbm, up_hbm, down_hbm) = refs_in
+    (out_block, out_dic) = refs_out
+    me = lax.axis_index("latent")
+    h = lax.axis_index("hidden")
+    other = 1 - h
+    rows, own_width = codes_x.shape
+    width = dic_hbm.shape[1]
+    units = dic_hbm.shape[0]
+    C = rows // ROWS
+    K = C // H
+    extra = K - L
+    n_dev = L * H
+    mine = me * H + h
+    pad = s.stage_x.shape[2]
+
+    def ext(hid):
+        return (2 + 3 * hid) % L
+
+    def at(lat, hid):
+        return {"latent": lat, "hidden": hid}
+
+    def rcopy(src, dst, ss, rs, lat, hid):
+        return pltpu.make_async_remote_copy(
+            src_ref=src, dst_ref=dst, send_sem=ss, recv_sem=rs,
+            device_id=at(lat, hid), device_id_type=MESH,
+        )
+
+    def each(n, body):
+        def step(i, carry):
+            body(i)
+            return carry
+
+        lax.fori_loop(0, n, step, 0)
+
+    def slots(body):
+        body(0, me)
+        if extra:
+            @pl.when(me == ext(h))
+            def _():
+                body(1, L)
+
+    loads = []
+    for i, (src, dst) in enumerate(
+        ((dic_hbm, s.dic), (down_hbm, s.down), (gate_hbm, s.gate), (up_hbm, s.up))
+    ):
+        cp = pltpu.make_async_copy(src, dst, s.load_sem.at[i])
+        cp.start()
+        loads.append(cp)
+
+    barrier = pltpu.get_barrier_semaphore()
+
+    def greet(j):
+        pl.semaphore_signal(barrier, inc=1, device_id=at(lax.rem(me + j, L), other), device_id_type=MESH)
+
+        @pl.when(j > 0)
+        def _():
+            pl.semaphore_signal(barrier, inc=1, device_id=at(lax.rem(me + j, L), h), device_id_type=MESH)
+
+    each(L, greet)
+
+    def stage(codes, buf):
+        value = codes[...].astype(F32) * (2.0 ** (-6))
+        value = jnp.concatenate([value, jnp.zeros((rows, pad - own_width), F32)], axis=1)
+        buf[...] = value.reshape(C, ROWS, pad).astype(BF16)
+
+    stage(codes_x, s.stage_x)
+    stage(codes_u, s.stage_u)
+    pl.semaphore_wait(barrier, n_dev - 1)
+
+    def turn_start(buf, arr, ss, rs):
+        def one(j):
+            lat = lax.rem(me + j, L)
+            for hid in range(H):
+                c = hid * K + lat
+                same = jnp.logical_and(lat == me, h == hid)
+
+                @pl.when(jnp.logical_not(same))
+                def _():
+                    rcopy(buf.at[c], arr.at[0, mine], ss.at[c], rs.at[0, mine], lat, hid).start()
+
+                @pl.when(same)
+                def _():
+                    arr[0, mine] = buf[c]
+
+        each(L, one)
+        if extra:
+            for hid in range(H):
+                c = hid * K + L
+                same = jnp.logical_and(ext(hid) == me, h == hid)
+
+                @pl.when(jnp.logical_not(same))
+                def _():
+                    rcopy(buf.at[c], arr.at[1, mine], ss.at[c], rs.at[1, mine], ext(hid), hid).start()
+
+                @pl.when(same)
+                def _():
+                    arr[1, mine] = buf[c]
+
+    def turn_finish(arr, rs, full):
+        def one(slot, k):
+            def get(i):
+                @pl.when(i != mine)
+                def _():
+                    rcopy(arr.at[slot, i], arr.at[slot, i], rs.at[slot, i], rs.at[slot, i], me, other).wait_recv()
+
+            each(n_dev, get)
+            pieces = [arr[slot, i].astype(F32)[:, :own_width] for i in range(n_dev)]
+            full[h * K + k] = jnp.concatenate(pieces, axis=1).astype(BF16)
+
+        slots(one)
+
+    def turn_drain(buf, ss):
+        def one(j):
+            lat = lax.rem(me + j, L)
+            for hid in range(H):
+                c = hid * K + lat
+
+                @pl.when(jnp.logical_not(jnp.logical_and(lat == me, h == hid)))
+                def _():
+                    rcopy(buf.at[c], buf.at[c], ss.at[c], ss.at[c], lat, hid).wait_send()
+
+        each(L, one)
+        if extra:
+            for hid in range(H):
+                c = hid * K + L
+
+                @pl.when(jnp.logical_not(jnp.logical_and(ext(hid) == me, h == hid)))
+                def _():
+                    rcopy(buf.at[c], buf.at[c], ss.at[c], ss.at[c], ext(hid), hid).wait_send()
+
+    X = 2
+    Z = L // X
+    z, x = me // X, lax.rem(me, X)
+    across_me = z * X + 1 - x
+
+    def peer(j):
+        if Z == 4:
+            return (z + 1 - 2 * lax.rem(z, 2), z + 2 - 4 * (z // 2), 3 - z)[j]
+        return lax.rem(z + 1 + j, Z)
+
+    def in_column(j):
+        return peer(j) * X + x
+
+    def beside(j):
+        return peer(j) * X + 1 - x
+
+    near = range(Z - 1)
+    far = (1, 2, 0) if Z == 4 else near
+    ext_here = lax.rem(ext(h), X) == x
+    ext_mine = me == ext(h)
+    ext_passes = jnp.logical_and(ext_here, jnp.logical_not(ext_mine))
+
+    def when_extra(cond, body):
+        if extra:
+            @pl.when(cond)
+            def _():
+                body(L)
+
+    def wait_here(buf, sem):
+        rcopy(buf, buf, sem, sem, me, other).wait_recv()
+
+    def wait_sent(buf, sem):
+        rcopy(buf, buf, sem, sem, me, other).wait_send()
+
+    def hand_over(full, a, k):
+        c = h * K + k
+        rcopy(full.at[c], full.at[c], s.ag_fs.at[a, k], s.ag_fr.at[a, k], me, other).start()
+
+    def step_across(full, a, k):
+        c = h * K + k
+        rcopy(full.at[c], full.at[c], s.ag_xs.at[a, k], s.ag_xr.at[a, k], across_me, h).start()
+
+    def spread_start(full, a):
+        def one(slot, k):
+            c = h * K + k
+            for j in far:
+                rcopy(full.at[c], full.at[c], s.ag_ss.at[a, slot, j], s.ag_rr.at[a, k], in_column(j), h).start()
+            step_across(full, a, k)
+            hand_over(full, a, k)
+
+        slots(one)
+
+    def relay_column(full, a, k):
+        wait_here(full.at[h * K + k], s.ag_rr.at[a, k])
+        step_across(full, a, k)
+        hand_over(full, a, k)
+
+    def relay_across(full, a, k):
+        wait_here(full.at[h * K + k], s.ag_xr.at[a, k])
+        hand_over(full, a, k)
+
+    def spread_column(full, a):
+        for j in near:
+            relay_column(full, a, in_column(j))
+        when_extra(ext_passes, lambda k: relay_column(full, a, k))
+
+    def spread_across(full, a):
+        relay_across(full, a, across_me)
+        for j in near:
+            relay_across(full, a, beside(j))
+        when_extra(jnp.logical_not(ext_here), lambda k: relay_across(full, a, k))
+
+    def spread_take(full, a):
+        each(K, lambda k: wait_here(full.at[other * K + k], s.ag_fr.at[a, k]))
+
+    def spread_drain(full, a):
+        def one(slot, k):
+            for j in near:
+                wait_sent(full.at[h * K + k], s.ag_ss.at[a, slot, j])
+
+        slots(one)
+        each(Z, lambda zz: wait_sent(full.at[h * K + zz * X + x], s.ag_xs.at[a, zz * X + x]))
+        when_extra(ext_here, lambda k: wait_sent(full.at[h * K + k], s.ag_xs.at[a, k]))
+        each(K, lambda k: wait_sent(full.at[h * K + k], s.ag_fs.at[a, k]))
+
+    def rows_of(full, dst):
+        dst[...] = full[...].astype(F32).reshape(rows, width).astype(BF16)
+
+    def sum_start(a):
+        def one(k):
+            c = other * K + k
+            rcopy(s.own.at[a, c], s.sib.at[a, k], s.rs_cs.at[a, k], s.rs_cr.at[a, k], me, other).start()
+
+        each(K, one)
+
+    def sum_chip(a, k):
+        wait_here(s.sib.at[a, k], s.rs_cr.at[a, k])
+        return s.own[a, h * K + k] + s.sib[a, k]
+
+    def sum_middle(a):
+        def leave(k):
+            s.comb[a, k] = sum_chip(a, k).astype(BF16)
+            rcopy(s.comb.at[a, k], s.xbuf.at[a, k], s.rs_xs.at[a, k], s.rs_xr.at[a, k], across_me, h).start()
+
+        for j in far:
+            leave(beside(j))
+        when_extra(jnp.logical_not(ext_here), leave)
+        leave(across_me)
+
+    def sum_cross(a):
+        def total(k):
+            value = sum_chip(a, k)
+            wait_here(s.xbuf.at[a, k], s.rs_xr.at[a, k])
+            return value + s.xbuf[a, k].astype(F32)
+
+        def leave(slot, k, owner):
+            s.comb[a, k] = total(k).astype(BF16)
+            rcopy(s.comb.at[a, k], s.rbuf.at[a, slot, z], s.rs_ss.at[a, k], s.rs_rr.at[a, slot, z], owner, h).start()
+
+        for j in far:
+            leave(0, in_column(j), in_column(j))
+        when_extra(ext_passes, lambda k: leave(1, k, ext(h)))
+        s.acc[a, 0] = total(me)
+
+        def keep(k):
+            s.acc[a, 1] = total(k)
+
+        when_extra(ext_mine, keep)
+
+    def sum_value(a, slot):
+        value = s.acc[a, slot]
+        for j in near:
+            wait_here(s.rbuf.at[a, slot, peer(j)], s.rs_rr.at[a, slot, peer(j)])
+            value = value + s.rbuf[a, slot, peer(j)].astype(F32)
+        return value
+
+    def sum_drain(a):
+        each(K, lambda k: wait_sent(s.sib.at[a, k], s.rs_cs.at[a, k]))
+        each(Z, lambda zz: wait_sent(s.xbuf.at[a, zz * X + 1 - x], s.rs_xs.at[a, zz * X + 1 - x]))
+        when_extra(jnp.logical_not(ext_here), lambda k: wait_sent(s.xbuf.at[a, k], s.rs_xs.at[a, k]))
+        for j in near:
+            wait_sent(s.xbuf.at[a, in_column(j)], s.rs_ss.at[a, in_column(j)])
+        when_extra(ext_passes, lambda k: wait_sent(s.xbuf.at[a, k], s.rs_ss.at[a, k]))
+
+    def put(a, cols, value):
+        s.own[a, :, :, cols] = value.reshape(C, ROWS, value.shape[1])
+
+    across = (((1,), (1,)), ((), ()))
+
+    def mm_t(x, w):
+        return lax.dot_general(x, w, across, preferred_element_type=F32)
+
+    def mm(x, w):
+        return lax.dot_general(x, w, (((1,), (0,)), ((), ())), preferred_element_type=F32)
+
+    def span(t, size):
+        return pl.ds(pl.multiple_of(t * size, size), size)
+
+    wide = TILE if width % TILE == 0 else LANES
+    deep = TILE if units % TILE == 0 else units
+    n_deep = units // deep
+
+    turn_start(s.stage_x, s.arr_x, s.tx_ss.at[0], s.tx_rs.at[0])
+    turn_start(s.stage_u, s.arr_u, s.tx_ss.at[1], s.tx_rs.at[1])
+    turn_finish(s.arr_x, s.tx_rs.at[0], s.full_x)
+    spread_start(s.full_x, 0)
+    turn_finish(s.arr_u, s.tx_rs.at[1], s.full_u)
+    spread_column(s.full_x, 0)
+    spread_start(s.full_u, 1)
+    spread_across(s.full_x, 0)
+    spread_take(s.full_x, 0)
+    rows_of(s.full_x, s.both_in.at[pl.ds(rows, rows)])
+    x_rows = s.both_in.at[pl.ds(rows, rows)]
+    loads[0].wait()
+    for t in range(n_deep):
+        cols = pl.ds(t * deep, deep)
+        pre = mm_t(x_rows[...], s.dic[cols, :]) + ebias[:, cols]
+        s.pre[:, cols] = pre
+        s.lat[:, cols] = jnp.maximum(pre, 0.0).astype(BF16)
+    spread_column(s.full_u, 1)
+    each(width // wide, lambda t: put(0, span(t, wide), mm(s.lat[...], s.dic[:, span(t, wide)])))
+    sum_start(0)
+    sum_middle(0)
+    spread_across(s.full_u, 1)
+    sum_cross(0)
+    spread_take(s.full_u, 1)
+    rows_of(s.full_u, s.u_rows)
+    loads[1].wait()
+    for t in range(n_deep):
+        cols = pl.ds(t * deep, deep)
+        s.hgrad[:, cols] = mm_t(s.u_rows[...], s.down[cols, :])
+
+    def norm(slot, k):
+        rebuilt = sum_value(0, slot) + dbias[...]
+        inverse = lax.rsqrt(jnp.sum(rebuilt * rebuilt, axis=1, keepdims=True) / width + 1e-06)
+        s.rebuilt[slot] = rebuilt
+        s.inverse[slot] = jnp.broadcast_to(inverse, (ROWS, LANES))
+        s.full_n[h * K + k] = (rebuilt * inverse * gain[...]).astype(BF16)
+
+    slots(norm)
+    spread_start(s.full_n, 2)
+    s.lat_t[:, :rows] = jnp.maximum(s.pre[...], 0.0).T.astype(BF16)
+    spread_column(s.full_n, 2)
+    spread_across(s.full_n, 2)
+    spread_take(s.full_n, 2)
+    rows_of(s.full_n, s.n_rows)
+    loads[2].wait()
+    loads[3].wait()
+    for t in range(n_deep):
+        cols = pl.ds(t * deep, deep)
+        g = mm_t(s.n_rows[...], s.gate[cols, :])
+        u = mm_t(s.n_rows[...], s.up[cols, :])
+        th = jnp.tanh(0.7978845608028654 * (g + 0.044715 * g * g * g))
+        value = 0.5 * g * (1.0 + th)
+        slope = 0.5 * (1.0 + th) + 0.5 * g * (1.0 - th * th) * 0.7978845608028654 * (
+            1.0 + 3.0 * 0.044715 * g * g
+        )
+        hg = s.hgrad[:, cols]
+        s.hid[:, cols] = (value * u).astype(BF16)
+        s.ggrad[:, cols] = (hg * u * slope).astype(BF16)
+        s.ugrad[:, cols] = (hg * value).astype(BF16)
+    each(
+        width // wide,
+        lambda t: put(
+            1,
+            span(t, wide),
+            mm(s.ggrad[...], s.gate[:, span(t, wide)]) + mm(s.ugrad[...], s.up[:, span(t, wide)]),
+        ),
+    )
+    sum_start(1)
+    sum_middle(1)
+    each(width // wide, lambda t: put(2, span(t, wide), mm(s.hid[...], s.down[:, span(t, wide)])))
+    sum_start(2)
+    sum_cross(1)
+    sum_middle(2)
+
+    def back(slot, k):
+        scaled = sum_value(1, slot) * gain[...]
+        rebuilt = s.rebuilt[slot]
+        inverse = s.inverse[slot][:, :1]
+        inner = jnp.sum(scaled * rebuilt, axis=1, keepdims=True)
+        target = s.full_x[h * K + k].astype(F32)
+        s.full_r[h * K + k] = (
+            inverse * scaled - inverse * inverse * inverse * rebuilt * (inner / width) + (rebuilt - target)
+        ).astype(BF16)
+
+    slots(back)
+    spread_start(s.full_r, 3)
+    spread_column(s.full_r, 3)
+    sum_cross(2)
+    spread_across(s.full_r, 3)
+    spread_take(s.full_r, 3)
+    rows_of(s.full_r, s.both_in.at[pl.ds(0, rows)])
+    r_rows = s.both_in.at[pl.ds(0, rows)]
+    for t in range(n_deep):
+        cols = pl.ds(t * deep, deep)
+        grad = mm_t(r_rows[...], s.dic[cols, :])
+        grad = jnp.where(s.pre[:, cols] > 0.0, grad, 0.0)
+        s.lat_t[cols, rows:] = grad.T.astype(BF16)
+
+    def turn_back(slot, k):
+        value = sum_value(2, slot)
+        c = h * K + k
+        for i in range(n_dev):
+            piece = value[:, i * own_width : (i + 1) * own_width]
+            piece = jnp.concatenate([piece, jnp.zeros((ROWS, pad - own_width), F32)], axis=1)
+            s.stage_o[slot, i] = piece.astype(BF16)
+
+        def send(i):
+            @pl.when(i != mine)
+            def _():
+                rcopy(s.stage_o.at[slot, i], s.arr_o.at[c], s.to_ss.at[slot, i], s.to_rs.at[c], i // H, lax.rem(i, H)).start()
+
+            @pl.when(i == mine)
+            def _():
+                s.arr_o[c] = s.stage_o[slot, i]
+
+        each(n_dev, send)
+
+    slots(turn_back)
+
+    def store(t):
+        return pltpu.make_async_copy(s.dgrad.at[:, span(t, wide)], out_dic.at[:, span(t, wide)], s.out_sem.at[t])
+
+    def last(t):
+        cols = span(t, wide)
+        s.dgrad[:, cols] = mm(s.lat_t[...], s.both_in[:, cols]).astype(BF16)
+        store(t).start()
+
+    each(width // wide, last)
+
+    def got(k):
+        for hid in range(H):
+            c = hid * K + k
+            is_mine = jnp.logical_and(h == hid, (ext(hid) if k is L else k) == me)
+
+            @pl.when(jnp.logical_not(is_mine))
+            def _():
+                rcopy(s.arr_o.at[c], s.arr_o.at[c], s.to_rs.at[c], s.to_rs.at[c], me, other).wait_recv()
+
+    each(L, got)
+    if extra:
+        got(L)
+    out_block[...] = s.arr_o[...].astype(F32).reshape(rows, pad)[:, :own_width].astype(BF16)
+
+    turn_drain(s.stage_x, s.tx_ss.at[0])
+    turn_drain(s.stage_u, s.tx_ss.at[1])
+    for a, full in enumerate((s.full_x, s.full_u, s.full_n, s.full_r)):
+        spread_drain(full, a)
+    for a in range(3):
+        sum_drain(a)
+
+    def out_gone(slot, k):
+        def one(i):
+            @pl.when(i != mine)
+            def _():
+                rcopy(s.stage_o.at[slot, i], s.stage_o.at[slot, i], s.to_ss.at[slot, i], s.to_ss.at[slot, i], me, other).wait_send()
+
+        each(n_dev, one)
+
+    slots(out_gone)
+    each(width // wide, lambda t: store(t).wait())
+
+
+def run_group(L, H, *args):
+    codes, dic = args[0], args[2]
+    rows, own_width = codes.shape
+    units, width = dic.shape
+    C = rows // ROWS
+    K = C // H
+    n_dev = L * H
+    pad = -(-own_width // LANES) * LANES
+    wide = TILE if width % TILE == 0 else LANES
+    V, D, R = pltpu.VMEM, pltpu.SemaphoreType.DMA, ROWS
+    scratch = dict(
+        dic=V((units, width), BF16), gate=V((units, width), BF16),
+        up=V((units, width), BF16), down=V((units, width), BF16),
+        stage_x=V((C, R, pad), BF16), stage_u=V((C, R, pad), BF16),
+        arr_x=V((2, n_dev, R, pad), BF16), arr_u=V((2, n_dev, R, pad), BF16),
+        full_x=V((C, R, width), BF16), full_u=V((C, R, width), BF16),
+        full_n=V((C, R, width), BF16), full_r=V((C, R, width), BF16),
+        both_in=V((2 * rows, width), BF16), u_rows=V((rows, width), BF16), n_rows=V((rows, width), BF16),
+        pre=V((rows, units), F32), hgrad=V((rows, units), F32),
+        lat=V((rows, units), BF16), hid=V((rows, units), BF16),
+        ggrad=V((rows, units), BF16), ugrad=V((rows, units), BF16),
+        lat_t=V((units, 2 * rows), BF16), dgrad=V((units, width), BF16),
+        own=V((3, C, R, width), F32), xbuf=V((3, K, R, width), BF16),
+        sib=V((3, K, R, width), F32), comb=V((3, K, R, width), BF16),
+        rbuf=V((3, 2, L // 2, R, width), BF16), acc=V((3, 2, R, width), F32),
+        rebuilt=V((2, R, width), F32), inverse=V((2, R, LANES), F32),
+        stage_o=V((2, n_dev, R, pad), BF16), arr_o=V((C, R, pad), BF16),
+        load_sem=D((4,)), out_sem=D((width // wide,)),
+        tx_ss=D((2, C)), tx_rs=D((2, 2, n_dev)),
+        ag_ss=D((4, 2, L // 2)), ag_xs=D((4, K)), ag_xr=D((4, K)), ag_rr=D((4, K)), ag_fs=D((4, K)), ag_fr=D((4, K)),
+        rs_cs=D((3, K)), rs_cr=D((3, K)), rs_ss=D((3, K)), rs_rr=D((3, 2, L // 2)), rs_xs=D((3, K)), rs_xr=D((3, K)),
+        to_ss=D((2, n_dev)), to_rs=D((C,)),
+    )
+    names = list(scratch)
+
+    def body(*refs):
+        group_kernel(L, H, refs[:9], refs[9:11], types.SimpleNamespace(**dict(zip(names, refs[11:]))))
+
+    any_spec = pl.BlockSpec(memory_space=pl.ANY)
+    vm = pl.BlockSpec(memory_space=pltpu.VMEM)
+    return pl.pallas_call(
+        body,
+        name="group_step",
+        out_shape=(
+            jax.ShapeDtypeStruct((rows, own_width), BF16),
+            jax.ShapeDtypeStruct((units, width), BF16),
+        ),
+        in_specs=[vm, vm, any_spec, vm, vm, vm, any_spec, any_spec, any_spec],
+        out_specs=(vm, any_spec),
+        scratch_shapes=[scratch[n] for n in names],
+        compiler_params=pltpu.CompilerParams(collective_id=0, has_side_effects=True, vmem_limit_bytes=60 * 2**20),
+    )(*args)
+
+
+def fits(L, H, rows, width, units, units_mlp):
+    if H != 2 or rows % (ROWS * H) or width % LANES or units % LANES or units != units_mlp:
+        return False
+    return L >= 6 and L % 2 == 0 and 0 <= rows // ROWS // H - L <= 1
+
 
 CODE_STEP = 2.0 ** (-6)
 NORM_EPSILON = 1e-06
@@ -32,6 +559,13 @@
     up_weight,
     down_weight,
 ):
+    L, H = lax.axis_size("latent"), lax.axis_size("hidden")
+    rows, width = input_codes.shape[0], dictionary.shape[1]
+    if fits(L, H, rows, width, dictionary.shape[0], gate_weight.shape[0]):
+        return run_group(
+            L, H, input_codes, cotangent_codes, dictionary, encoder_bias[None, :], decoder_bias[None, :],
+            norm_gain[None, :], gate_weight, up_weight, down_weight,
+        )
     own_width = input_codes.shape[1]
     model_width = own_width * lax.axis_size(("latent", "hidden"))
     cotangent_local = (cotangent_codes.astype(jnp.float32) * CODE_STEP).astype(jnp.bfloat16)

time: 310 us -> 87 us (0.28)
  waiting for transfers between devices: 203 us -> 0 us
  Pallas kernels: 0 us -> 78.7 us
  blocking collectives: 50.9 us -> 0 us
  matrix products: 26.4 us -> 0 us
  between operations: 13.9 us -> 0.64 us
  other arithmetic: 7.82 us -> 0 us
    psum x2 -> x0, waiting for transfers between devices: 151 us -> none  [the longest x1 88.4 us: per_device(): scaled = lax.psum(partial_grad, ('latent', 'hidden')) * norm_gain]
    pallas_call x0 -> x1, Pallas kernels: none -> 78.7 us  [run_group(): pl.pallas_call(body, name='group_step', out_shape=(jax.ShapeDtypeStruct((...]
    unnamed x4 -> x0, waiting for transfers between devices: 51.5 us -> none
    all_gather x2 -> x0, blocking collectives: 50.9 us -> none  [the longest x1 26.4 us: per_device(): lax.all_gather(inputs_local, ('latent', 'hidden'), axis=1, tiled=True)]
    dot_general x9 -> x0, matrix products: 22 us -> none  [the longest x1 5.08 us: per_device(): lax.dot_general(preact_grad, inputs, DOWNWARD, preferred_element_type=jnp...]
    unnamed x1 -> x0, matrix products: 4.35 us -> none
    reduce_sum x2 -> x0, other arithmetic: 3.78 us -> none  [the longest x1 2.13 us: per_device(): inner_row = jnp.sum(scaled * rebuilt, axis=1, keepdims=True)]
    convert_element_type x3 -> x0, other arithmetic: 3.46 us -> none  [the longest x1 2.52 us: per_device(): rebuilt_grad = (inverse * scaled - inverse_cube * rebuilt * (inner_row /...]
  transfers between devices with their start and end apart: 3 -> 0, of which waited for: 3 -> 0; matrix products, arithmetic and copies ran while one was open for 9% -> 0% of each run, Pallas kernels for 0% -> 0%
where the time goes in v1:
time: 87 us; the launch traced here: 86.7 us
  Pallas kernels  78.7 us (90%)
  local copies, waits for them, and re-layouts  7.37 us (8%)
    pallas_call x1, Pallas kernels, run_group(): pl.pallas_call(body, name='group_step', out_shape=(jax.ShapeDtypeStruct((...  78.7 us
    unnamed x2, local copies, waits for them, and re-layouts  4.74 us

profile of v1, /device:TPU:0, one launch (start us, length us, event | category | flops | bytes accessed | tf_op | source)
XLA Modules:
  0.0 86.7 jit_solution(5833212714417047622)
XLA Ops:
  0.6 1.3 %broadcast_in_dim.10.refs_4_ = f32[1,2304]{1,0:T(1,128)} reshape(f32[2304]{0:T(1024)} %param.13) | data formatting | bytes 18432 | tf_op jit(solution)/shard_map/broadcast_in_dim | solution.py:566
  1.9 1.3 %broadcast_in_dim.11.refs_5_ = f32[1,2304]{1,0:T(1,128)} reshape(f32[2304]{0:T(1024)} %param.14) | data formatting | bytes 18432 | tf_op jit(solution)/shard_map/broadcast_in_dim | solution.py:567
  3.3 78.7 %group_step.1 = (bf16[144,144]{1,0:T(8,128)(2,1)}, bf16[512,2304]{1,0:T(8,128)(2,1)}) custom-call(s32[144,144]{1,0:T(8,128)} %refs_0_.1, s32[144,144]{1,0:T(8,128)} %refs_1_.1, bf16[512,2304]{1,0:T(8,128)(2,1)} %refs_2_.1, f32[1,512]{1,0:T(1,128)} %bitcast.1, f32[1,2304]{1,0:T(1,128)} %broadcast_in_dim.10.refs_4_, f32[1,2304]{1,0:T(1,128)} %broadcast_in_dim.11.refs_5_, ...), custom_call_target="tpu_custom_call" | custom-call | tf_op jit(solution)/shard_map/group_step/pallas_call | solution.py:513
  81.9 1.5 %copy.13 = bf16[144,144]{1,0:T(8,128)(2,1)} copy(bf16[144,144]{1,0:T(8,128)(2,1)} %get-tuple-element.4) | data formatting | bytes 82944
  83.4 3.2 %copy.14 = bf16[512,2304]{1,0:T(8,128)(2,1)} copy(bf16[512,2304]{1,0:T(8,128)(2,1)} %get-tuple-element.5) | data formatting | bytes 4718592

commit v2 on v1

--- a/solution.py
+++ b/solution.py
@@ -17,7 +17,7 @@
 
 def group_kernel(L, H, refs_in, refs_out, s):
     (codes_x, codes_u, dic_hbm, ebias, dbias, gain, gate_hbm, up_hbm, down_hbm) = refs_in
-    (out_block, out_dic) = refs_out
+    (out_cols, out_left, out_right) = refs_out
     me = lax.axis_index("latent")
     h = lax.axis_index("hidden")
     other = 1 - h
@@ -234,15 +234,22 @@
     def rows_of(full, dst):
         dst[...] = full[...].astype(F32).reshape(rows, width).astype(BF16)
 
+    def span(t, size):
+        return pl.ds(pl.multiple_of(t * size, size), size)
+
+    wide = TILE if width % TILE == 0 else LANES
+    def sum_tile(a, t, value):
+        cols = span(t, wide)
+        s.own[a, :, :, cols] = value.reshape(C, ROWS, wide)
+        rcopy(
+            s.own.at[a, pl.ds(other * K, K), :, cols], s.sib.at[a, :, :, cols],
+            s.rs_cs.at[a, t], s.rs_cr.at[a, t], me, other,
+        ).start()
+
     def sum_start(a):
-        def one(k):
-            c = other * K + k
-            rcopy(s.own.at[a, c], s.sib.at[a, k], s.rs_cs.at[a, k], s.rs_cr.at[a, k], me, other).start()
-
-        each(K, one)
+        each(width // wide, lambda t: wait_here(s.sib.at[a, :, :, span(t, wide)], s.rs_cr.at[a, t]))
 
     def sum_chip(a, k):
-        wait_here(s.sib.at[a, k], s.rs_cr.at[a, k])
         return s.own[a, h * K + k] + s.sib[a, k]
 
     def sum_middle(a):
@@ -283,16 +290,13 @@
         return value
 
     def sum_drain(a):
-        each(K, lambda k: wait_sent(s.sib.at[a, k], s.rs_cs.at[a, k]))
+        each(width // wide, lambda t: wait_sent(s.sib.at[a, :, :, span(t, wide)], s.rs_cs.at[a, t]))
         each(Z, lambda zz: wait_sent(s.xbuf.at[a, zz * X + 1 - x], s.rs_xs.at[a, zz * X + 1 - x]))
         when_extra(jnp.logical_not(ext_here), lambda k: wait_sent(s.xbuf.at[a, k], s.rs_xs.at[a, k]))
         for j in near:
             wait_sent(s.xbuf.at[a, in_column(j)], s.rs_ss.at[a, in_column(j)])
         when_extra(ext_passes, lambda k: wait_sent(s.xbuf.at[a, k], s.rs_ss.at[a, k]))
 
-    def put(a, cols, value):
-        s.own[a, :, :, cols] = value.reshape(C, ROWS, value.shape[1])
-
     across = (((1,), (1,)), ((), ()))
 
     def mm_t(x, w):
@@ -301,10 +305,6 @@
     def mm(x, w):
         return lax.dot_general(x, w, (((1,), (0,)), ((), ())), preferred_element_type=F32)
 
-    def span(t, size):
-        return pl.ds(pl.multiple_of(t * size, size), size)
-
-    wide = TILE if width % TILE == 0 else LANES
     deep = TILE if units % TILE == 0 else units
     n_deep = units // deep
 
@@ -319,6 +319,12 @@
     spread_take(s.full_x, 0)
     rows_of(s.full_x, s.both_in.at[pl.ds(rows, rows)])
     x_rows = s.both_in.at[pl.ds(rows, rows)]
+
+    def store_right(part):
+        at_rows = pl.ds(part * rows, rows)
+        return pltpu.make_async_copy(s.both_in.at[at_rows], out_right.at[at_rows], s.out_sem.at[part])
+
+    store_right(1).start()
     loads[0].wait()
     for t in range(n_deep):
         cols = pl.ds(t * deep, deep)
@@ -326,7 +332,7 @@
         s.pre[:, cols] = pre
         s.lat[:, cols] = jnp.maximum(pre, 0.0).astype(BF16)
     spread_column(s.full_u, 1)
-    each(width // wide, lambda t: put(0, span(t, wide), mm(s.lat[...], s.dic[:, span(t, wide)])))
+    each(width // wide, lambda t: sum_tile(0, t, mm(s.lat[...], s.dic[:, span(t, wide)])))
     sum_start(0)
     sum_middle(0)
     spread_across(s.full_u, 1)
@@ -369,18 +375,19 @@
         s.ugrad[:, cols] = (hg * value).astype(BF16)
     each(
         width // wide,
-        lambda t: put(
+        lambda t: sum_tile(
             1,
-            span(t, wide),
+            t,
             mm(s.ggrad[...], s.gate[:, span(t, wide)]) + mm(s.ugrad[...], s.up[:, span(t, wide)]),
         ),
     )
     sum_start(1)
     sum_middle(1)
-    each(width // wide, lambda t: put(2, span(t, wide), mm(s.hid[...], s.down[:, span(t, wide)])))
+    each(width // wide, lambda t: sum_tile(2, t, mm(s.hid[...], s.down[:, span(t, wide)])))
     sum_start(2)
     sum_cross(1)
     sum_middle(2)
+    sum_cross(2)
 
     def back(slot, k):
         scaled = sum_value(1, slot) * gain[...]
@@ -392,20 +399,6 @@
             inverse * scaled - inverse * inverse * inverse * rebuilt * (inner / width) + (rebuilt - target)
         ).astype(BF16)
 
-    slots(back)
-    spread_start(s.full_r, 3)
-    spread_column(s.full_r, 3)
-    sum_cross(2)
-    spread_across(s.full_r, 3)
-    spread_take(s.full_r, 3)
-    rows_of(s.full_r, s.both_in.at[pl.ds(0, rows)])
-    r_rows = s.both_in.at[pl.ds(0, rows)]
-    for t in range(n_deep):
-        cols = pl.ds(t * deep, deep)
-        grad = mm_t(r_rows[...], s.dic[cols, :])
-        grad = jnp.where(s.pre[:, cols] > 0.0, grad, 0.0)
-        s.lat_t[cols, rows:] = grad.T.astype(BF16)
-
     def turn_back(slot, k):
         value = sum_value(2, slot)
         c = h * K + k
@@ -425,17 +418,23 @@
 
         each(n_dev, send)
 
+    slots(back)
+    spread_start(s.full_r, 3)
+    spread_column(s.full_r, 3)
+    spread_across(s.full_r, 3)
     slots(turn_back)
-
-    def store(t):
-        return pltpu.make_async_copy(s.dgrad.at[:, span(t, wide)], out_dic.at[:, span(t, wide)], s.out_sem.at[t])
-
-    def last(t):
-        cols = span(t, wide)
-        s.dgrad[:, cols] = mm(s.lat_t[...], s.both_in[:, cols]).astype(BF16)
-        store(t).start()
-
-    each(width // wide, last)
+    spread_take(s.full_r, 3)
+    rows_of(s.full_r, s.both_in.at[pl.ds(0, rows)])
+    r_rows = s.both_in.at[pl.ds(0, rows)]
+    store_right(0).start()
+    for t in range(n_deep):
+        cols = pl.ds(t * deep, deep)
+        grad = mm_t(r_rows[...], s.dic[cols, :])
+        grad = jnp.where(s.pre[:, cols] > 0.0, grad, 0.0)
+        s.lat_t[cols, rows:] = grad.T.astype(BF16)
+
+    store_left = pltpu.make_async_copy(s.lat_t, out_left, s.out_sem.at[2])
+    store_left.start()
 
     def got(k):
         for hid in range(H):
@@ -449,7 +448,7 @@
     each(L, got)
     if extra:
         got(L)
-    out_block[...] = s.arr_o[...].astype(F32).reshape(rows, pad)[:, :own_width].astype(BF16)
+    out_cols[...] = s.arr_o[...]
 
     turn_drain(s.stage_x, s.tx_ss.at[0])
     turn_drain(s.stage_u, s.tx_ss.at[1])
@@ -467,7 +466,9 @@
         each(n_dev, one)
 
     slots(out_gone)
-    each(width // wide, lambda t: store(t).wait())
+    store_left.wait()
+    for part in (0, 1):
+        store_right(part).wait()
 
 
 def run_group(L, H, *args):
@@ -491,37 +492,65 @@
         pre=V((rows, units), F32), hgrad=V((rows, units), F32),
         lat=V((rows, units), BF16), hid=V((rows, units), BF16),
         ggrad=V((rows, units), BF16), ugrad=V((rows, units), BF16),
-        lat_t=V((units, 2 * rows), BF16), dgrad=V((units, width), BF16),
+        lat_t=V((units, 2 * rows), BF16),
         own=V((3, C, R, width), F32), xbuf=V((3, K, R, width), BF16),
         sib=V((3, K, R, width), F32), comb=V((3, K, R, width), BF16),
         rbuf=V((3, 2, L // 2, R, width), BF16), acc=V((3, 2, R, width), F32),
         rebuilt=V((2, R, width), F32), inverse=V((2, R, LANES), F32),
         stage_o=V((2, n_dev, R, pad), BF16), arr_o=V((C, R, pad), BF16),
-        load_sem=D((4,)), out_sem=D((width // wide,)),
+        load_sem=D((4,)), out_sem=D((3,)),
         tx_ss=D((2, C)), tx_rs=D((2, 2, n_dev)),
         ag_ss=D((4, 2, L // 2)), ag_xs=D((4, K)), ag_xr=D((4, K)), ag_rr=D((4, K)), ag_fs=D((4, K)), ag_fr=D((4, K)),
-        rs_cs=D((3, K)), rs_cr=D((3, K)), rs_ss=D((3, K)), rs_rr=D((3, 2, L // 2)), rs_xs=D((3, K)), rs_xr=D((3, K)),
+        rs_cs=D((3, width // wide)), rs_cr=D((3, width // wide)), rs_ss=D((3, K)), rs_rr=D((3, 2, L // 2)), rs_xs=D((3, K)), rs_xr=D((3, K)),
         to_ss=D((2, n_dev)), to_rs=D((C,)),
     )
     names = list(scratch)
 
     def body(*refs):
-        group_kernel(L, H, refs[:9], refs[9:11], types.SimpleNamespace(**dict(zip(names, refs[11:]))))
+        group_kernel(L, H, refs[:9], refs[9:12], types.SimpleNamespace(**dict(zip(names, refs[12:]))))
 
     any_spec = pl.BlockSpec(memory_space=pl.ANY)
     vm = pl.BlockSpec(memory_space=pltpu.VMEM)
-    return pl.pallas_call(
+    cols, left, right = pl.pallas_call(
         body,
         name="group_step",
+        out_shape=(
+            jax.ShapeDtypeStruct((C, R, pad), BF16),
+            jax.ShapeDtypeStruct((units, 2 * rows), BF16),
+            jax.ShapeDtypeStruct((2 * rows, width), BF16),
+        ),
+        in_specs=[vm, vm, any_spec, vm, vm, vm, any_spec, any_spec, any_spec],
+        out_specs=(vm, any_spec, any_spec),
+        scratch_shapes=[scratch[n] for n in names],
+        compiler_params=pltpu.CompilerParams(collective_id=0, has_side_effects=True, vmem_limit_bytes=60 * 2**20),
+    )(*args)
+
+    def product(cols, left, right, block, grad):
+        grad[...] = jnp.dot(left[...], right[...], preferred_element_type=F32).astype(BF16)
+
+        @pl.when(pl.program_id(0) == 0)
+        def _():
+            block[...] = cols[...].astype(F32).reshape(rows, pad)[:, :own_width].astype(BF16)
+
+    step = width // 3 if width % (3 * LANES) == 0 else wide
+    return pl.pallas_call(
+        product,
+        name="dictionary_product",
+        grid=(width // step,),
         out_shape=(
             jax.ShapeDtypeStruct((rows, own_width), BF16),
             jax.ShapeDtypeStruct((units, width), BF16),
         ),
-        in_specs=[vm, vm, any_spec, vm, vm, vm, any_spec, any_spec, any_spec],
-        out_specs=(vm, any_spec),
-        scratch_shapes=[scratch[n] for n in names],
-        compiler_params=pltpu.CompilerParams(collective_id=0, has_side_effects=True, vmem_limit_bytes=60 * 2**20),
-    )(*args)
+        in_specs=[
+            pl.BlockSpec((C, R, pad), lambda t: (0, 0, 0)),
+            pl.BlockSpec((units, 2 * rows), lambda t: (0, 0)),
+            pl.BlockSpec((2 * rows, step), lambda t: (0, t)),
+        ],
+        out_specs=(
+            pl.BlockSpec((rows, own_width), lambda t: (0, 0)),
+            pl.BlockSpec((units, step), lambda t: (0, t)),
+        ),
+    )(cols, left, right)
 
 
 def fits(L, H, rows, width, units, units_mlp):
@@ -563,8 +592,8 @@
     rows, width = input_codes.shape[0], dictionary.shape[1]
     if fits(L, H, rows, width, dictionary.shape[0], gate_weight.shape[0]):
         return run_group(
-            L, H, input_codes, cotangent_codes, dictionary, encoder_bias[None, :], decoder_bias[None, :],
-            norm_gain[None, :], gate_weight, up_weight, down_weight,
+            L, H, input_codes, cotangent_codes, dictionary, encoder_bias[None, :], decoder_bias,
+            norm_gain, gate_weight, up_weight, down_weight,
         )
     own_width = input_codes.shape[1]
     model_width = own_width * lax.axis_size(("latent", "hidden"))

time: 87 us -> 82.3 us (0.946)
  local copies, waits for them, and re-layouts: 7.37 us -> 0 us
  Pallas kernels: 78.7 us -> 81.5 us
    unnamed x2 -> x0, local copies, waits for them, and re-layouts: 4.74 us -> none
    pallas_call x0 -> x1, Pallas kernels: none -> 4.51 us  [run_group(): pl.pallas_call(product, name='dictionary_product', grid=(width // step,),...]
    broadcast_in_dim x2 -> x0, local copies, waits for them, and re-layouts: 2.62 us -> none  [the longest x1 1.31 us: per_device(): decoder_bias[None, :]]
    pallas_call x1, Pallas kernels: 78.7 us -> 76.9 us  [run_group(): pl.pallas_call(body, name='group_step', out_shape=(jax.ShapeDtypeStruct((...]
where the time goes in v2:
time: 82.3 us; the launch traced here: 82.1 us
  Pallas kernels  81.5 us (99%)
    pallas_call x1, Pallas kernels, run_group(): pl.pallas_call(body, name='group_step', out_shape=(jax.ShapeDtypeStruct((...  76.9 us
    pallas_call x1, Pallas kernels, run_group(): pl.pallas_call(product, name='dictionary_product', grid=(width // step,),...  4.51 us

profile of v2, /device:TPU:0, one launch (start us, length us, event | category | flops | bytes accessed | tf_op | source)
XLA Modules:
  0.0 82.1 jit_solution(6761863077284338477)
XLA Ops:
  0.6 76.9 %group_step.1 = (bf16[18,8,256]{2,1,0:T(8,128)(2,1)}, bf16[512,288]{1,0:T(8,128)(2,1)}, bf16[288,2304]{1,0:T(8,128)(2,1)}) custom-call(s32[144,144]{1,0:T(8,128)} %refs_0_.1, s32[144,144]{1,0:T(8,128)} %refs_1_.1, bf16[512,2304]{1,0:T(8,128)(2,1)} %refs_2_.1, f32[1,512]{1,0:T(1,128)} %bitcast.1, f32[2304]{0:T(1024)} %refs_4_.1, f32[2304]{0:T(1024)} %refs_5_.1, ...), custom_call_target="tpu_custom_call" | custom-call | tf_op jit(solution)/shard_map/group_step/pallas_call | solution.py:514
  77.6 4.5 %dictionary_product.1 = (bf16[144,144]{1,0:T(8,128)(2,1)}, bf16[512,2304]{1,0:T(8,128)(2,1)}) custom-call(bf16[18,8,256]{2,1,0:T(8,128)(2,1)} %get-tuple-element.5.cols, bf16[512,288]{1,0:T(8,128)(2,1)} %get-tuple-element.6.left, bf16[288,2304]{1,0:T(8,128)(2,1)} %get-tuple-element.7.right), custom_call_target="tpu_custom_call" | custom-call | tf_op jit(solution)/shard_map/dictionary_product/pallas_call | solution.py:536

commit v3 on v2

--- a/solution.py
+++ b/solution.py
@@ -235,7 +235,7 @@
         dst[...] = full[...].astype(F32).reshape(rows, width).astype(BF16)
 
     def span(t, size):
-        return pl.ds(pl.multiple_of(t * size, size), size)
+        return pl.ds(t * size if isinstance(t, int) else pl.multiple_of(t * size, size), size)
 
     wide = TILE if width % TILE == 0 else LANES
     def sum_tile(a, t, value):
@@ -246,21 +246,35 @@
             s.rs_cs.at[a, t], s.rs_cr.at[a, t], me, other,
         ).start()
 
-    def sum_start(a):
-        each(width // wide, lambda t: wait_here(s.sib.at[a, :, :, span(t, wide)], s.rs_cr.at[a, t]))
-
     def sum_chip(a, k):
         return s.own[a, h * K + k] + s.sib[a, k]
 
-    def sum_middle(a):
+    def sum_across(a, t):
+        cols = span(t, wide)
+        wait_here(s.sib.at[a, :, :, cols], s.rs_cr.at[a, t])
+
         def leave(k):
-            s.comb[a, k] = sum_chip(a, k).astype(BF16)
-            rcopy(s.comb.at[a, k], s.xbuf.at[a, k], s.rs_xs.at[a, k], s.rs_xr.at[a, k], across_me, h).start()
+            s.comb[a, k, :, cols] = (s.own[a, h * K + k, :, cols] + s.sib[a, k, :, cols]).astype(BF16)
+            rcopy(
+                s.comb.at[a, k, :, cols], s.xbuf.at[a, k, :, cols],
+                s.rs_xs.at[a, k], s.rs_xr.at[a, k], across_me, h,
+            ).start()
 
         for j in far:
             leave(beside(j))
         when_extra(jnp.logical_not(ext_here), leave)
         leave(across_me)
+
+    def sum_loop(a, make):
+        def one(t):
+            sum_tile(a, t, make(t))
+
+            @pl.when(t > 0)
+            def _():
+                sum_across(a, t - 1)
+
+        each(width // wide, one)
+        sum_across(a, width // wide - 1)
 
     def sum_cross(a):
         def total(k):
@@ -332,9 +346,7 @@
         s.pre[:, cols] = pre
         s.lat[:, cols] = jnp.maximum(pre, 0.0).astype(BF16)
     spread_column(s.full_u, 1)
-    each(width // wide, lambda t: sum_tile(0, t, mm(s.lat[...], s.dic[:, span(t, wide)])))
-    sum_start(0)
-    sum_middle(0)
+    sum_loop(0, lambda t: mm(s.lat[...], s.dic[:, span(t, wide)]))
     spread_across(s.full_u, 1)
     sum_cross(0)
     spread_take(s.full_u, 1)
@@ -373,20 +385,12 @@
         s.hid[:, cols] = (value * u).astype(BF16)
         s.ggrad[:, cols] = (hg * u * slope).astype(BF16)
         s.ugrad[:, cols] = (hg * value).astype(BF16)
-    each(
-        width // wide,
-        lambda t: sum_tile(
-            1,
-            t,
-            mm(s.ggrad[...], s.gate[:, span(t, wide)]) + mm(s.ugrad[...], s.up[:, span(t, wide)]),
-        ),
-    )
-    sum_start(1)
-    sum_middle(1)
-    each(width // wide, lambda t: sum_tile(2, t, mm(s.hid[...], s.down[:, span(t, wide)])))
-    sum_start(2)
+    sum_loop(
+        1,
+        lambda t: mm(s.ggrad[...], s.gate[:, span(t, wide)]) + mm(s.ugrad[...], s.up[:, span(t, wide)]),
+    )
+    sum_loop(2, lambda t: mm(s.hid[...], s.down[:, span(t, wide)]))
     sum_cross(1)
-    sum_middle(2)
     sum_cross(2)
 
     def back(slot, k):

time: 82.3 us -> 91.2 us (1.11)
  Pallas kernels: 81.5 us -> 90.4 us
    pallas_call x1, Pallas kernels: 76.9 us -> 85.8 us  [run_group(): pl.pallas_call(body, name='group_step', out_shape=(jax.ShapeDtypeStruct((...]
where the time goes in v3:
time: 91.2 us; the launch traced here: 91 us
  Pallas kernels  90.4 us (99%)
    pallas_call x1, Pallas kernels, run_group(): pl.pallas_call(body, name='group_step', out_shape=(jax.ShapeDtypeStruct((...  85.8 us
    pallas_call x1, Pallas kernels, run_group(): pl.pallas_call(product, name='dictionary_product', grid=(width // step,),...  4.51 us

profile of v3, /device:TPU:0, one launch (start us, length us, event | category | flops | bytes accessed | tf_op | source)
XLA Modules:
  0.0 91.0 jit_solution(3702713756245128092)
XLA Ops:
  0.6 85.8 %group_step.1 = (bf16[18,8,256]{2,1,0:T(8,128)(2,1)}, bf16[512,288]{1,0:T(8,128)(2,1)}, bf16[288,2304]{1,0:T(8,128)(2,1)}) custom-call(s32[144,144]{1,0:T(8,128)} %refs_0_.1, s32[144,144]{1,0:T(8,128)} %refs_1_.1, bf16[512,2304]{1,0:T(8,128)(2,1)} %refs_2_.1, f32[1,512]{1,0:T(1,128)} %bitcast.1, f32[2304]{0:T(1024)} %refs_4_.1, f32[2304]{0:T(1024)} %refs_5_.1, ...), custom_call_target="tpu_custom_call" | custom-call | tf_op jit(solution)/shard_map/group_step/pallas_call | solution.py:518
  86.5 4.5 %dictionary_product.1 = (bf16[144,144]{1,0:T(8,128)(2,1)}, bf16[512,2304]{1,0:T(8,128)(2,1)}) custom-call(bf16[18,8,256]{2,1,0:T(8,128)(2,1)} %get-tuple-element.5.cols, bf16[512,288]{1,0:T(8,128)(2,1)} %get-tuple-element.6.left, bf16[288,2304]{1,0:T(8,128)(2,1)} %get-tuple-element.7.right), custom_call_target="tpu_custom_call" | custom-call | tf_op jit(solution)/shard_map/dictionary_product/pallas_call | solution.py:540

commit v4 on v2

--- a/solution.py
+++ b/solution.py
@@ -237,7 +237,7 @@
     def span(t, size):
         return pl.ds(pl.multiple_of(t * size, size), size)
 
-    wide = TILE if width % TILE == 0 else LANES
+    wide = 3 * TILE if width % (3 * TILE) == 0 else LANES
     def sum_tile(a, t, value):
         cols = span(t, wide)
         s.own[a, :, :, cols] = value.reshape(C, ROWS, wide)
@@ -479,7 +479,7 @@
     K = C // H
     n_dev = L * H
     pad = -(-own_width // LANES) * LANES
-    wide = TILE if width % TILE == 0 else LANES
+    wide = 3 * TILE if width % (3 * TILE) == 0 else LANES
     V, D, R = pltpu.VMEM, pltpu.SemaphoreType.DMA, ROWS
     scratch = dict(
         dic=V((units, width), BF16), gate=V((units, width), BF16),

time: 82.3 us -> 80.2 us (0.974)
  Pallas kernels: 81.5 us -> 79.4 us
    pallas_call x1, Pallas kernels: 76.9 us -> 74.8 us  [run_group(): pl.pallas_call(body, name='group_step', out_shape=(jax.ShapeDtypeStruct((...]
where the time goes in v4:
time: 80.2 us; the launch traced here: 80 us
  Pallas kernels  79.4 us (99%)
    pallas_call x1, Pallas kernels, run_group(): pl.pallas_call(body, name='group_step', out_shape=(jax.ShapeDtypeStruct((...  74.8 us
    pallas_call x1, Pallas kernels, run_group(): pl.pallas_call(product, name='dictionary_product', grid=(width // step,),...  4.51 us

profile of v4, /device:TPU:0, one launch (start us, length us, event | category | flops | bytes accessed | tf_op | source)
XLA Modules:
  0.0 80.0 jit_solution(17865088838138463439)
XLA Ops:
  0.6 74.8 %group_step.1 = (bf16[18,8,256]{2,1,0:T(8,128)(2,1)}, bf16[512,288]{1,0:T(8,128)(2,1)}, bf16[288,2304]{1,0:T(8,128)(2,1)}) custom-call(s32[144,144]{1,0:T(8,128)} %refs_0_.1, s32[144,144]{1,0:T(8,128)} %refs_1_.1, bf16[512,2304]{1,0:T(8,128)(2,1)} %refs_2_.1, f32[1,512]{1,0:T(1,128)} %bitcast.1, f32[2304]{0:T(1024)} %refs_4_.1, f32[2304]{0:T(1024)} %refs_5_.1, ...), custom_call_target="tpu_custom_call" | custom-call | tf_op jit(solution)/shard_map/group_step/pallas_call | solution.py:514
  75.5 4.5 %dictionary_product.1 = (bf16[144,144]{1,0:T(8,128)(2,1)}, bf16[512,2304]{1,0:T(8,128)(2,1)}) custom-call(bf16[18,8,256]{2,1,0:T(8,128)(2,1)} %get-tuple-element.5.cols, bf16[512,288]{1,0:T(8,128)(2,1)} %get-tuple-element.6.left, bf16[288,2304]{1,0:T(8,128)(2,1)} %get-tuple-element.7.right), custom_call_target="tpu_custom_call" | custom-call | tf_op jit(solution)/shard_map/dictionary_product/pallas_call | solution.py:536
